TPU v7x, 32 devices: a whole 2x2x4 slice. The times are simulated.
32 devices in a mesh: tp: 4 (over y, x), row: 4 (over z), col: 2 (over core).
Axes of the slice: x: 2, y: 2, z: 4, core: 2. Of those that a mesh axis runs over, the one named last changes fastest.
Arguments:
- hidden: bfloat16 [128, 14336], P('col', 'row'), may hold values from -6 to 6
- out_grad: bfloat16 [128, 4096], P(None, ('tp', 'row')), may hold values from -6 to 6
- basis_in: bfloat16 [14336, 4096], P(('row', 'col'), 'tp'), may hold values from -0.046875 to 0.046875
- basis_out: bfloat16 [4096, 1024], P(('tp', 'row'), 'col'), may hold values from -0.09375 to 0.09375
- eigen: float32 [4096, 1024], P(('tp', 'row'), 'col'), may hold values from 0.02 to 2
Outputs:
- precond: float32 [4096, 14336], P(('tp', 'col'), 'row')
All inputs are finite; a program needn't handle non-finite values.
Results may differ from a plain program's by a relative error of at most 0.024.
Values may be sent and summed in bfloat16 or wider, within the bound.
No kernel may reach another device: no remote copies, remote signals or barrier semaphores. Data moves between devices by JAX's collectives and lax.ppermute only.
A program may use at most 64 MiB of HBM per device.

v0:
```python
import jax
import jax.numpy as jnp
from jax import lax
from jax.sharding import PartitionSpec as P

damping = 0.01


def contract_rows(left, right):
    return lax.dot_general(
        left, right, (((0,), (0,)), ((), ())), preferred_element_type=jnp.float32
    )


def contract_cols(left, right):
    return lax.dot_general(
        left, right, (((1,), (1,)), ((), ())), preferred_element_type=jnp.float32
    )


def shards(hidden, out_grad, basis_in, basis_out, eigen):
    tp_count = lax.axis_size("tp")
    col_count = lax.axis_size("col")
    basis_block = lax.all_gather(basis_in, "col", axis=0, tiled=True)
    partial_in = jnp.dot(hidden, basis_block, preferred_element_type=jnp.float32)
    rotated_in = lax.psum_scatter(
        partial_in.astype(jnp.bfloat16), "row", scatter_dimension=1, tiled=True
    )
    rotated_in = lax.all_gather(rotated_in, "col", axis=0, tiled=True)
    queries = rotated_in.shape[0]
    partial_out = jnp.dot(out_grad, basis_out, preferred_element_type=jnp.float32)
    rotated_out = lax.psum(partial_out, ("tp", "row")).astype(jnp.bfloat16)
    coeff = contract_rows(rotated_in, rotated_out)
    scaled = (coeff / (queries * (eigen + damping))).astype(jnp.bfloat16)
    mixed_part = contract_cols(scaled, lax.all_gather(basis_out, ("tp", "row"), axis=0, tiled=True))
    depth = mixed_part.shape[0]
    width = mixed_part.shape[1]
    mixed_part = mixed_part.reshape(depth, tp_count, col_count, width // (tp_count * col_count))
    mixed = lax.psum_scatter(
        mixed_part.astype(jnp.bfloat16), "col", scatter_dimension=2, tiled=True
    ).astype(jnp.float32)
    mixed = mixed.reshape(depth, width // col_count).astype(jnp.bfloat16)
    mixed = lax.all_gather(mixed, "row", axis=0, tiled=True)
    return lax.psum_scatter(
        lax.dot_general(
            mixed, basis_block, (((0,), (1,)), ((), ())), preferred_element_type=jnp.float32
        ).astype(jnp.bfloat16),
        "tp",
        scatter_dimension=0,
        tiled=True,
    ).astype(jnp.float32)


def solution(mesh):
    placed = (
        P("col", "row"),
        P(None, ("tp", "row")),
        P(("row", "col"), "tp"),
        P(("tp", "row"), "col"),
        P(("tp", "row"), "col"),
    )
    return jax.shard_map(
        shards, mesh=mesh, in_specs=placed, out_specs=P(("tp", "col"), "row"), check_vma=False
    )
```

profile of v0, /device:TPU:0, one launch (start us, length us, event | category | flops | bytes accessed | tf_op | source)
XLA Modules:
  0.0 397.8 jit_solution(9604397828768367093)
XLA Ops:
  7.4 0.0 copy-start
  7.4 0.0 all-gather.4.cloned.1.call-start
  7.4 0.7 all-gather.4.cloned.1.call-update
  8.1 0.0 copy-start.1
  8.1 0.0 copy-start.2
  8.1 0.0 copy-start.3
  8.1 0.0 reduce-scatter.4.cloned.1.call-start
  8.2 22.6 %all-gather.4.cloned.1.call-done = bf16[3584,1024]{1,0:T(8,128)(2,1)} async-done(((bf16[1792,1024]{1,0:T(8,128)(2,1)}), bf16[3584,1024]{1,0:T(8,128)(2,1)}) %all-gather.4.cloned.1.call-update) | async-done | bytes 7340048 | tf_op jit(solution)/shard_map/all_gather | solution.py:24
  30.8 0.0 copy-done
  30.8 5.1 %convolution_convert_fusion.2 = bf16[64,1024]{1,0:T(8,128)(2,1)} fusion(bf16[64,3584]{1,0:T(8,128)(2,1)S(1)} %copy-done, bf16[3584,1024]{1,0:T(8,128)(2,1)} %all-gather.4.cloned.1.call-done), kind=kOutput, calls=%fused_computation.4 | convolution fusion | flops 469827584 | bytes 7929856 | tf_op jit(solution)/shard_map/dot_general | solution.py:25
  35.9 0.0 reduce-scatter.4.cloned.1.call-update
  35.9 0.0 all-gather.6.cloned.1.call-start
  36.0 0.5 all-gather.6.cloned.1.call-update
  36.5 0.0 reduce-scatter.6.cloned.1.call-start
  36.5 0.0 copy-done.1
  36.6 0.0 copy-done.2
  36.6 0.2 fusion.9
  36.8 85.1 %all-reduce.1 = bf16[128,512]{1,0:T(8,128)(2,1)S(1)} all-reduce(f32[128,512]{1,0:T(8,128)S(1)} %fusion.9), channel_id=1, replica_groups=mesh['tp'=4,'row'=4,'col'=2] {'tp','row'}, use_global_device_ids=true, to_apply=%region_1.0 | all-reduce | flops 65536 | bytes 393216 | tf_op jit(solution)/shard_map/psum | solution.py:32
  121.9 0.0 reduce-scatter.4.cloned.1.call-done
  121.9 2.1 all_gather.13
  124.0 0.0 all-gather.6.cloned.1.call-done
  124.0 0.0 copy-done.3
  124.0 4.9 %convolution_convert_fusion.1 = bf16[256,4096]{1,0:T(8,128)(2,1)} fusion(bf16[4096,512]{1,0:T(8,128)(2,1)} %all-gather.6.cloned.1.call-done, bf16[128,256]{1,0:T(8,128)(2,1)S(1)} %all_gather.13, f32[256,512]{1,0:T(8,128)S(1)} %copy-done.3, bf16[128,512]{1,0:T(8,128)(2,1)S(1)} %all-reduce.1), kind=kOutput, calls=%fused_computation.1 | convolution fusion | flops 1108869120 | bytes 7012352 | tf_op jit(solution)/shard_map/dot_general | solution.py:16
  128.9 3.3 convert_element_type.30
  132.2 4.1 %copy.6 = bf16[256,4,2,512]{0,3,1,2:T(8,128)(2,1)} copy(bf16[256,4,2,512]{3,2,1,0:T(2,128)(2,1)S(1)} %convert_element_type.30) | data formatting | bytes 4194304 | tf_op jit(solution)/shard_map/convert_element_type | solution.py:40
  136.3 0.0 reduce-scatter.6.cloned.1.call-update
  136.4 0.0 all-gather.8.cloned.1.call-start
  136.4 6.9 %reduce-scatter.6.cloned.1.call-done = bf16[256,4,1,512]{0,3,1,2:T(8,128)(2,1)} async-done(((bf16[256,4,2,512]{0,3,1,2:T(8,128)(2,1)}), bf16[256,4,1,512]{0,3,1,2:T(8,128)(2,1)}) %reduce-scatter.6.cloned.1.call-update) | async-done | bytes 1048592 | tf_op jit(solution)/shard_map/reduce_scatter | solution.py:39
  143.3 0.0 all-gather.8.cloned.1.call-update
  143.4 0.0 reduce-scatter.8.cloned.1.call-start
  143.4 83.2 %all-gather.8.cloned.1.call-done = bf16[1024,2048]{0,1:T(8,128)(2,1)} async-done(((bf16[256,2048]{0,1:T(8,128)(2,1)}), bf16[1024,2048]{0,1:T(8,128)(2,1)}) %all-gather.8.cloned.1.call-update) | async-done | bytes 4194320 | tf_op jit(solution)/shard_map/all_gather | solution.py:43
  226.6 22.0 %convolution_convert_fusion = bf16[2048,3584]{1,0:T(8,128)(2,1)} fusion(bf16[1024,2048]{0,1:T(8,128)(2,1)} %all-gather.8.cloned.1.call-done, bf16[3584,1024]{1,0:T(8,128)(2,1)} %all-gather.4.cloned.1.call-done), kind=kOutput, calls=%fused_computation | convolution fusion | flops 15039725568 | bytes 26214400 | tf_op jit(solution)/shard_map/dot_general | solution.py:45
  248.6 0.0 reduce-scatter.8.cloned.1.call-update
  248.7 135.9 %reduce-scatter.8.cloned.1.call-done = bf16[512,3584]{1,0:T(8,128)(2,1)} async-done(((bf16[2048,3584]{1,0:T(8,128)(2,1)}), bf16[512,3584]{1,0:T(8,128)(2,1)}) %reduce-scatter.8.cloned.1.call-update) | async-done | bytes 3670032 | tf_op jit(solution)/shard_map/reduce_scatter | solution.py:44
  384.6 6.0 %convert_element_type.33 = f32[512,3584]{1,0:T(8,128)} convert(bf16[512,3584]{1,0:T(8,128)(2,1)} %reduce-scatter.8.cloned.1.call-done) | non-fusion elementwise | flops 1835008 | bytes 11010048 | tf_op jit(solution)/shard_map/convert_element_type | solution.py:51
Async XLA Ops:
  7.4 23.4 %copy-start = (bf16[64,3584]{1,0:T(8,128)(2,1)S(1)}, bf16[64,3584]{1,0:T(8,128)(2,1)}, u32[]{:S(2)}) copy-start(bf16[64,3584]{1,0:T(8,128)(2,1)} %param.5) | copy-start | bytes 1376260
  7.4 23.4 %all-gather.4.cloned.1.call-start = ((), (), s32[]{:S(2)}) async-start(), calls=%async_computation.3 | async-start | bytes 11010048 | tf_op jit(solution)/shard_map/all_gather | solution.py:24
  8.1 28.5 %copy-start.1 = (bf16[256,512]{1,0:T(8,128)(2,1)S(1)}, bf16[256,512]{1,0:T(8,128)(2,1)}, u32[]{:S(2)}) copy-start(bf16[256,512]{1,0:T(8,128)(2,1)} %param.8) | copy-start | bytes 786436
  8.1 28.5 %copy-start.2 = (bf16[128,256]{1,0:T(8,128)(2,1)S(1)}, bf16[128,256]{1,0:T(8,128)(2,1)}, u32[]{:S(2)}) copy-start(bf16[128,256]{1,0:T(8,128)(2,1)} %param.6) | copy-start | bytes 196612
  8.1 115.9 %copy-start.3 = (f32[256,512]{1,0:T(8,128)S(1)}, f32[256,512]{1,0:T(8,128)}, u32[]{:S(2)}) copy-start(f32[256,512]{1,0:T(8,128)} %param.9) | copy-start | bytes 1572868
  8.1 113.8 %reduce-scatter.4.cloned.1.call-start = ((), (), s32[]{:S(2)}) async-start(), calls=%async_computation.4 | async-start | bytes 163840 | tf_op jit(solution)/shard_map/reduce_scatter | solution.py:26
  35.9 88.1 %all-gather.6.cloned.1.call-start = ((), (), s32[]{:S(2)}) async-start(), calls=%async_computation.5 | async-start | bytes 4456448 | tf_op jit(solution)/shard_map/all_gather | solution.py:35
  36.5 106.8 %reduce-scatter.6.cloned.1.call-start = ((), (), s32[]{:S(2)}) async-start(), calls=%async_computation.6 | async-start | bytes 3145728 | tf_op jit(solution)/shard_map/reduce_scatter | solution.py:39
  136.4 90.2 %all-gather.8.cloned.1.call-start = ((), (), s32[]{:S(2)}) async-start(), calls=%async_computation.7 | async-start | bytes 5242880 | tf_op jit(solution)/shard_map/all_gather | solution.py:43
  143.4 241.2 %reduce-scatter.8.cloned.1.call-start = ((), (), s32[]{:S(2)}) async-start(), calls=%async_computation.8 | async-start | bytes 18350080 | tf_op jit(solution)/shard_map/reduce_scatter | solution.py:44
Sparse Core Ops, SparseCore 0:
  9.7 21.0 all-gather.3
  36.0 21.2 reduce-scatter.3
  136.5 6.8 reduce-scatter.5
  144.7 81.7 all-gather.7
Sparse Core Ops, SparseCore 1:
  39.2 78.1 all-gather.5
  248.7 135.8 reduce-scatter.7
where the time goes:
time: 398 us
  waiting for transfers between devices  250 us (63%)
  blocking collectives  87.2 us (22%)
  matrix products  32.3 us (8%)
  between operations  14.7 us (4%)
  local copies, waits for them, and re-layouts  7.4 us (2%)
  other arithmetic  6.04 us (2%)
    reduce_scatter x1, waiting for transfers between devices, shards(): lax.psum_scatter(lax.dot_general(mixed, basis_block, (((0,), (1,)), ((),...  136 us
    psum x1, blocking collectives, shards(): rotated_out = lax.psum(partial_out, ('tp', 'row')).astype(jnp.bfloat16)  85.1 us
    all_gather x1, waiting for transfers between devices, shards(): mixed = lax.all_gather(mixed, 'row', axis=0, tiled=True)  83.2 us
    all_gather x1, waiting for transfers between devices, shards(): basis_block = lax.all_gather(basis_in, 'col', axis=0, tiled=True)  22.6 us
    dot_general x1, matrix products, shards(): lax.dot_general(mixed, basis_block, (((0,), (1,)), ((), ())), preferred_e...  22 us
  transfers between devices with their start and end apart: 6, of which 4 were waited for; matrix products, arithmetic and copies ran while one was open for 0% of the time, Pallas kernels for 0%

commit v1 on v0

--- a/solution.py
+++ b/solution.py
@@ -29,7 +29,7 @@
     rotated_in = lax.all_gather(rotated_in, "col", axis=0, tiled=True)
     queries = rotated_in.shape[0]
     partial_out = jnp.dot(out_grad, basis_out, preferred_element_type=jnp.float32)
-    rotated_out = lax.psum(partial_out, ("tp", "row")).astype(jnp.bfloat16)
+    rotated_out = jnp.sum(lax.all_gather(partial_out, ("tp", "row")), axis=0).astype(jnp.bfloat16)
     coeff = contract_rows(rotated_in, rotated_out)
     scaled = (coeff / (queries * (eigen + damping))).astype(jnp.bfloat16)
     mixed_part = contract_cols(scaled, lax.all_gather(basis_out, ("tp", "row"), axis=0, tiled=True))

time: 398 us -> 468 us (1.18)
  waiting for transfers between devices: 250 us -> 402 us
  blocking collectives: 87.2 us -> 2.05 us
    psum x1 -> x0, blocking collectives: 85.1 us -> none  [shards(): rotated_out = lax.psum(partial_out, ('tp', 'row')).astype(jnp.bfloat16)]
    all_gather x1, waiting for transfers between devices: 0.01 us -> 74.1 us  [shards(): lax.all_gather(basis_out, ('tp', 'row'), axis=0, tiled=True)]
    all_gather x0 -> x1, waiting for transfers between devices: none -> 56.7 us  [shards(): lax.all_gather(partial_out, ('tp', 'row'))]
    reduce_scatter x1, waiting for transfers between devices: 0.02 us -> 19.6 us  [shards(): lax.psum_scatter(partial_in.astype(jnp.bfloat16), 'row', scatter_dimensio...]
  transfers between devices with their start and end apart: 6 -> 7, of which waited for: 4 -> 7; matrix products, arithmetic and copies ran while one was open for 0% -> 1% of each run, Pallas kernels for 0% -> 0%
where the time goes in v1:
time: 468 us
  waiting for transfers between devices  402 us (86%)
  matrix products  33 us (7%)
  between operations  14.9 us (3%)
  other arithmetic  8.68 us (2%)
  local copies, waits for them, and re-layouts  7.4 us (2%)
    reduce_scatter x1, waiting for transfers between devices, shards(): lax.psum_scatter(lax.dot_general(mixed, basis_block, (((0,), (1,)), ((),...  136 us
    all_gather x1, waiting for transfers between devices, shards(): mixed = lax.all_gather(mixed, 'row', axis=0, tiled=True)  83.2 us
    all_gather x1, waiting for transfers between devices, shards(): lax.all_gather(basis_out, ('tp', 'row'), axis=0, tiled=True)  74.1 us
    all_gather x1, waiting for transfers between devices, shards(): lax.all_gather(partial_out, ('tp', 'row'))  56.7 us
    all_gather x1, waiting for transfers between devices, shards(): basis_block = lax.all_gather(basis_in, 'col', axis=0, tiled=True)  22.6 us
    dot_general x1, matrix products, shards(): lax.dot_general(mixed, basis_block, (((0,), (1,)), ((), ())), preferred_e...  22 us
    reduce_scatter x1, waiting for transfers between devices, shards(): lax.psum_scatter(partial_in.astype(jnp.bfloat16), 'row', scatter_dimensio...  19.6 us
  transfers between devices with their start and end apart: 7, of which 7 were waited for; matrix products, arithmetic and copies ran while one was open for 1% of the time, Pallas kernels for 0%

profile of v1, /device:TPU:0, one launch (start us, length us, event | category | flops | bytes accessed | tf_op | source)
XLA Modules:
  0.0 468.1 jit_solution(6623680096974001339)
XLA Ops:
  7.4 0.0 copy-start
  7.4 0.0 all-gather.6.cloned.1.call-start
  7.4 0.7 all-gather.6.cloned.1.call-update
  8.1 0.0 copy-start.1
  8.1 0.0 copy-start.2
  8.1 0.0 reduce-scatter.4.cloned.1.call-start
  8.2 22.6 %all-gather.6.cloned.1.call-done = bf16[3584,1024]{1,0:T(8,128)(2,1)} async-done(((bf16[1792,1024]{1,0:T(8,128)(2,1)}), bf16[3584,1024]{1,0:T(8,128)(2,1)}) %all-gather.6.cloned.1.call-update) | async-done | bytes 7340048 | tf_op jit(solution)/shard_map/all_gather | solution.py:24
  30.8 0.0 copy-done
  30.8 5.1 %convolution_convert_fusion.2 = bf16[64,1024]{1,0:T(8,128)(2,1)} fusion(bf16[64,3584]{1,0:T(8,128)(2,1)S(1)} %copy-done, bf16[3584,1024]{1,0:T(8,128)(2,1)} %all-gather.6.cloned.1.call-done), kind=kOutput, calls=%fused_computation.4 | convolution fusion | flops 469827584 | bytes 7929856 | tf_op jit(solution)/shard_map/dot_general | solution.py:25
  35.9 0.0 copy-start.3
  35.9 0.0 reduce-scatter.4.cloned.1.call-update
  35.9 0.0 all-gather.12.cloned.1.call-start
  36.0 0.0 copy-done.1
  36.0 0.0 copy-done.2
  36.0 0.9 fusion.9
  36.9 0.0 all-gather.12.cloned.1.call-update
  36.9 0.0 all-gather.8.cloned.1.call-start
  37.0 0.5 all-gather.8.cloned.1.call-update
  37.5 0.0 reduce-scatter.6.cloned.1.call-start
  37.5 19.6 %reduce-scatter.4.cloned.1.call-done = bf16[64,256]{1,0:T(8,128)(2,1)} async-done(((bf16[64,1024]{1,0:T(8,128)(2,1)}), bf16[64,256]{1,0:T(8,128)(2,1)}) %reduce-scatter.4.cloned.1.call-update) | async-done | bytes 32784 | tf_op jit(solution)/shard_map/reduce_scatter | solution.py:26
  57.1 2.1 all_gather.19
  59.2 56.7 %all-gather.12.cloned.1.call-done = f32[2048,512]{1,0:T(8,128)} async-done(((f32[128,512]{1,0:T(8,128)}), f32[2048,512]{1,0:T(8,128)}) %all-gather.12.cloned.1.call-update) | async-done | bytes 4194320 | tf_op jit(solution)/shard_map/all_gather | solution.py:32
  115.9 2.6 reduce_sum.9
  118.5 74.1 %all-gather.8.cloned.1.call-done = bf16[4096,512]{1,0:T(8,128)(2,1)} async-done(((bf16[256,512]{1,0:T(8,128)(2,1)}), bf16[4096,512]{1,0:T(8,128)(2,1)}) %all-gather.8.cloned.1.call-update) | async-done | bytes 4194320 | tf_op jit(solution)/shard_map/all_gather | solution.py:35
  192.6 0.0 copy-done.3
  192.6 4.9 %convolution_convert_fusion.1 = bf16[256,4096]{1,0:T(8,128)(2,1)} fusion(bf16[4096,512]{1,0:T(8,128)(2,1)} %all-gather.8.cloned.1.call-done, bf16[128,256]{1,0:T(8,128)(2,1)S(1)} %all_gather.19, f32[256,512]{1,0:T(8,128)S(1)} %copy-done.3, bf16[128,512]{1,0:T(8,128)(2,1)S(1)} %reduce_sum.9), kind=kOutput, calls=%fused_computation.1 | convolution fusion | flops 1108869120 | bytes 7012352 | tf_op jit(solution)/shard_map/dot_general | solution.py:16
  197.5 3.3 convert_element_type.30
  200.8 4.1 copy.6
  204.9 0.0 reduce-scatter.6.cloned.1.call-update
  204.9 0.0 all-gather.10.cloned.1.call-start
  205.0 8.5 %reduce-scatter.6.cloned.1.call-done = bf16[256,4,1,512]{0,3,1,2:T(8,128)(2,1)} async-done(((bf16[256,4,2,512]{0,3,1,2:T(8,128)(2,1)}), bf16[256,4,1,512]{0,3,1,2:T(8,128)(2,1)}) %reduce-scatter.6.cloned.1.call-update) | async-done | bytes 1048592 | tf_op jit(solution)/shard_map/reduce_scatter | solution.py:39
  213.4 0.0 all-gather.10.cloned.1.call-update
  213.5 0.0 reduce-scatter.8.cloned.1.call-start
  213.5 83.2 %all-gather.10.cloned.1.call-done = bf16[1024,2048]{0,1:T(8,128)(2,1)} async-done(((bf16[256,2048]{0,1:T(8,128)(2,1)}), bf16[1024,2048]{0,1:T(8,128)(2,1)}) %all-gather.10.cloned.1.call-update) | async-done | bytes 4194320 | tf_op jit(solution)/shard_map/all_gather | solution.py:43
  296.7 22.0 %convolution_convert_fusion = bf16[2048,3584]{1,0:T(8,128)(2,1)} fusion(bf16[1024,2048]{0,1:T(8,128)(2,1)} %all-gather.10.cloned.1.call-done, bf16[3584,1024]{1,0:T(8,128)(2,1)} %all-gather.6.cloned.1.call-done), kind=kOutput, calls=%fused_computation | convolution fusion | flops 15039725568 | bytes 26214400 | tf_op jit(solution)/shard_map/dot_general | solution.py:45
  318.7 0.0 reduce-scatter.8.cloned.1.call-update
  318.8 135.9 %reduce-scatter.8.cloned.1.call-done = bf16[512,3584]{1,0:T(8,128)(2,1)} async-done(((bf16[2048,3584]{1,0:T(8,128)(2,1)}), bf16[512,3584]{1,0:T(8,128)(2,1)}) %reduce-scatter.8.cloned.1.call-update) | async-done | bytes 3670032 | tf_op jit(solution)/shard_map/reduce_scatter | solution.py:44
  454.7 6.0 %convert_element_type.33 = f32[512,3584]{1,0:T(8,128)} convert(bf16[512,3584]{1,0:T(8,128)(2,1)} %reduce-scatter.8.cloned.1.call-done) | non-fusion elementwise | flops 1835008 | bytes 11010048 | tf_op jit(solution)/shard_map/convert_element_type | solution.py:51
Async XLA Ops:
  7.4 23.4 %copy-start = (bf16[64,3584]{1,0:T(8,128)(2,1)S(1)}, bf16[64,3584]{1,0:T(8,128)(2,1)}, u32[]{:S(2)}) copy-start(bf16[64,3584]{1,0:T(8,128)(2,1)} %param.5) | copy-start | bytes 1376260
  7.4 23.4 %all-gather.6.cloned.1.call-start = ((), (), s32[]{:S(2)}) async-start(), calls=%async_computation.3 | async-start | bytes 11010048 | tf_op jit(solution)/shard_map/all_gather | solution.py:24
  8.1 27.9 %copy-start.1 = (bf16[256,512]{1,0:T(8,128)(2,1)S(1)}, bf16[256,512]{1,0:T(8,128)(2,1)}, u32[]{:S(2)}) copy-start(bf16[256,512]{1,0:T(8,128)(2,1)} %param.8) | copy-start | bytes 786436
  8.1 27.9 %copy-start.2 = (bf16[128,256]{1,0:T(8,128)(2,1)S(1)}, bf16[128,256]{1,0:T(8,128)(2,1)}, u32[]{:S(2)}) copy-start(bf16[128,256]{1,0:T(8,128)(2,1)} %param.6) | copy-start | bytes 196612
  8.1 49.0 %reduce-scatter.4.cloned.1.call-start = ((), (), s32[]{:S(2)}) async-start(), calls=%async_computation.4 | async-start | bytes 163840 | tf_op jit(solution)/shard_map/reduce_scatter | solution.py:26
  35.9 156.7 %copy-start.3 = (f32[256,512]{1,0:T(8,128)S(1)}, f32[256,512]{1,0:T(8,128)}, u32[]{:S(2)}) copy-start(f32[256,512]{1,0:T(8,128)} %param.9) | copy-start | bytes 1572868
  35.9 79.9 %all-gather.12.cloned.1.call-start = ((), (), s32[]{:S(2)}) async-start(), calls=%async_computation.9 | async-start | bytes 4456448 | tf_op jit(solution)/shard_map/all_gather | solution.py:32
  36.9 155.7 %all-gather.8.cloned.1.call-start = ((), (), s32[]{:S(2)}) async-start(), calls=%async_computation.5 | async-start | bytes 4456448 | tf_op jit(solution)/shard_map/all_gather | solution.py:35
  37.5 175.9 %reduce-scatter.6.cloned.1.call-start = ((), (), s32[]{:S(2)}) async-start(), calls=%async_computation.6 | async-start | bytes 3145728 | tf_op jit(solution)/shard_map/reduce_scatter | solution.py:39
  204.9 91.8 %all-gather.10.cloned.1.call-start = ((), (), s32[]{:S(2)}) async-start(), calls=%async_computation.7 | async-start | bytes 5242880 | tf_op jit(solution)/shard_map/all_gather | solution.py:43
  213.5 241.2 %reduce-scatter.8.cloned.1.call-start = ((), (), s32[]{:S(2)}) async-start(), calls=%async_computation.8 | async-start | bytes 18350080 | tf_op jit(solution)/shard_map/reduce_scatter | solution.py:44
Sparse Core Ops, SparseCore 0:
  9.7 21.0 all-gather.5
  36.0 21.0 reduce-scatter.3
  205.0 8.3 reduce-scatter.5
  214.8 81.8 all-gather.9
Sparse Core Ops, SparseCore 1:
  39.2 76.6 all-gather.11
  118.5 74.0 all-gather.7
  318.8 135.8 reduce-scatter.7
